TPU v7x, 32 devices: a whole 2x2x4 slice. The times are simulated.
32 devices in a mesh: fsdp: 8 (over y, x, core), blk: 4 (over z).
Axes of the slice: x: 2, y: 2, z: 4, core: 2. Of those that a mesh axis runs over, the one named last changes fastest.
Arguments:
- grad: bfloat16 [16, 768, 768], P(None, 'fsdp', 'blk'), may hold values from -16 to 16
- owner_slots: int32 [16], replicated, may hold values from 0 to 15, as said below
- stat_left: float32 [16, 768, 768], P('fsdp', None, 'blk'), may hold values from -6 to 6
- stat_right: float32 [16, 768, 768], P('fsdp', None, 'blk'), may hold values from -6 to 6
- basis_left: bfloat16 [16, 768, 768], P('fsdp'), may hold values from -1 to 1, as said below
- basis_right: bfloat16 [16, 768, 768], P('fsdp'), may hold values from -1 to 1, as said below
- moment: float32 [16, 768, 768], P('fsdp', None, 'blk'), may hold values from -3 to 3
- second: float32 [16, 768, 768], P('fsdp', None, 'blk'), may hold values from 0.01 to 0.1
Outputs:
- update: bfloat16 [16, 768, 768], P(None, 'fsdp', 'blk')
- new_left: float32 [16, 768, 768], P('fsdp', None, 'blk')
- new_right: float32 [16, 768, 768], P('fsdp', None, 'blk')
- new_moment: float32 [16, 768, 768], P('fsdp', None, 'blk')
- new_second: float32 [16, 768, 768], P('fsdp', None, 'blk')
- grad_rms: float32 [], replicated
Inputs may be any that keep to these rules, and one draw needn't show every extreme that they name: Each 768 x 768 block of basis_left is orthogonal up to bfloat16 rounding. Each 768 x 768 block of basis_right is orthogonal up to bfloat16 rounding. owner_slots names every block exactly once.
All inputs are finite; a program needn't handle non-finite values.
Results may differ from a plain program's by a relative error of at most 0.0058.
Values may be sent and summed in bfloat16 or wider, within the bound.
No kernel may reach another device: no remote copies, remote signals or barrier semaphores. Data moves between devices by JAX's collectives and lax.ppermute only.
A program may use at most 64 MiB of HBM per device.

v0:
```python
import jax
import jax.numpy as jnp
from jax import lax
from jax.sharding import PartitionSpec as P

BS = 768
clip_level = 0.5
stat_decay = 0.95
beta_one = 0.9
beta_two = 0.95
epsilon = 1e-08


def body(grad, owner_slots, stat_left, stat_right, basis_left, basis_right, moment, second):
    arranged = jnp.take(grad, owner_slots, axis=0)
    owned = lax.all_to_all(arranged, "fsdp", split_axis=0, concat_axis=1, tiled=True)
    width = owned.shape[2]
    first_col = lax.axis_index("blk") * width
    entries = grad.shape[0] * BS * BS
    partial_sum = jnp.sum(jnp.square(owned.astype(jnp.float32)))
    total = lax.psum(partial_sum, ("fsdp", "blk"))
    grad_rms = jnp.sqrt(total / entries)
    factor = jnp.minimum(1.0, clip_level / grad_rms)
    whole = lax.all_gather(owned, "blk", axis=2, tiled=True)
    own_rows = lax.dynamic_slice_in_dim(whole, first_col, width, 1)
    right_cols = lax.dynamic_slice_in_dim(basis_right, first_col, width, 2)
    outer_left = jnp.einsum("bij,bkj->bik", whole, own_rows, preferred_element_type=jnp.float32)
    outer_right = jnp.einsum("bji,bjk->bik", whole, owned, preferred_element_type=jnp.float32)
    new_left = stat_decay * stat_left + (1.0 - stat_decay) * (factor * factor) * outer_left
    new_right = stat_decay * stat_right + (1.0 - stat_decay) * (factor * factor) * outer_right
    turned = jnp.einsum(
        "bij,bjk->bik", whole, right_cols, preferred_element_type=jnp.float32
    ).astype(jnp.bfloat16)
    rotated = factor * jnp.einsum(
        "bji,bjk->bik", basis_left, turned, preferred_element_type=jnp.float32
    )
    new_moment = beta_one * moment + (1.0 - beta_one) * rotated
    new_second = beta_two * second + (1.0 - beta_two) * rotated * rotated
    scaled = (new_moment / (jnp.sqrt(new_second) + epsilon)).astype(jnp.bfloat16)
    back = jnp.einsum(
        "bij,bjk->bik", basis_left, scaled, preferred_element_type=jnp.float32
    ).astype(jnp.bfloat16)
    right_rows = lax.dynamic_slice_in_dim(basis_right, first_col, width, 1)
    summed = jnp.einsum(
        "bij,bkj->bik",
        lax.all_gather(back, "blk", axis=2, tiled=True),
        right_rows,
        preferred_element_type=jnp.float32,
    )
    stepped = summed.astype(jnp.bfloat16)
    returned = lax.all_to_all(stepped, "fsdp", split_axis=1, concat_axis=0, tiled=True)
    placed = jnp.zeros_like(returned).at[owner_slots].set(returned)
    return (placed, new_left, new_right, new_moment, new_second, grad_rms)


def solution(mesh):
    placed = (
        P(None, "fsdp", "blk"),
        P(),
        P("fsdp", None, "blk"),
        P("fsdp", None, "blk"),
        P("fsdp", None, None),
        P("fsdp", None, None),
        P("fsdp", None, "blk"),
        P("fsdp", None, "blk"),
    )
    return jax.shard_map(
        body,
        mesh=mesh,
        in_specs=placed,
        out_specs=(
            P(None, "fsdp", "blk"),
            P("fsdp", None, "blk"),
            P("fsdp", None, "blk"),
            P("fsdp", None, "blk"),
            P("fsdp", None, "blk"),
            P(),
        ),
        check_vma=False,
    )
```

profile of v0, /device:TPU:0, one launch (start us, length us, event | category | flops | bytes accessed | tf_op | source)
XLA Modules:
  0.0 176.2 jit_solution(13508039111027429911)
XLA Ops:
  7.2 0.0 copy-start
  7.2 0.0 all-gather.3.cloned.1.call-start
  7.2 0.8 compare_select_fusion
  8.0 0.7 compare_and_fusion
  8.7 1.7 gather_fusion
  10.4 0.1 broadcast_select_fusion
  10.6 17.6 %all_to_all.36 = bf16[16,96,192]{2,1,0:T(8,128)(2,1)} all-to-all(bf16[16,96,192]{2,1,0:T(8,128)(2,1)S(1)} %broadcast_select_fusion), channel_id=1, replica_groups=mesh['fsdp'=8,'blk'=4] {'fsdp'}, dimensions={0} | all-to-all | bytes 1179648 | tf_op jit(solution)/shard_map/all_to_all | solution.py:16
  28.2 1.6 copy.24
  29.8 1.5 all_to_all.29
  31.2 2.5 %copy.25 = bf16[2,768,192]{1,0,2:T(2,128)(2,1)} copy(bf16[2,768,192]{1,2,0:T(8,128)(2,1)} %all_to_all.29) | data formatting | bytes 1179648 | tf_op jit(solution)/shard_map/all_to_all | solution.py:16
  33.7 0.0 all-gather.3.cloned.1.call-update
  33.8 0.0 all-gather.5.cloned.1.call-start
  33.8 1.0 multiply_reduce_fusion
  34.8 43.4 %psum.7 = f32[]{:T(128)} all-reduce(f32[]{:T(128)} %multiply_reduce_fusion), channel_id=1, replica_groups=mesh['fsdp'=8,'blk'=4] {'fsdp','blk'}, use_global_device_ids=true, to_apply=%region_1.2 | all-reduce | flops 1 | bytes 8 | tf_op jit(solution)/shard_map/psum | solution.py:21
  79.0 5.3 %all-gather.3.cloned.1.call-done = bf16[2,768,768]{1,0,2:T(2,128)(2,1)} async-done(((bf16[2,768,192]{1,0,2:T(2,128)(2,1)}), bf16[2,768,768]{1,0,2:T(2,128)(2,1)}) %all-gather.3.cloned.1.call-update) | async-done | bytes 2359312 | tf_op jit(solution)/shard_map/all_gather | solution.py:24
  84.3 0.0 copy-done
  84.3 5.2 %fusion.25 = (f32[2,768,192]{1,2,0:T(8,128)S(1)}, f32[2,768,192]{1,2,0:T(8,128)}) fusion(f32[2,768,192]{1,2,0:T(8,128)} %param.15, f32[2,768,192]{1,2,0:T(8,128)} %param.14, bf16[2,768,768]{2,1,0:T(8,128)(2,1)S(1)} %copy-done, bf16[2,768,768]{1,0,2:T(2,128)(2,1)} %all-gather.3.cloned.1.call-done, bf16[2,768,768]{2,1,0:T(8,128)(2,1)} %param.13, ...), kind=kOutput, calls=%fused_computation.20 | convolution fusion | flops 908623872 | bytes 10223624 | tf_op jit(solution)/shard_map/bji,bjk->bik/dot_general | solution.py:34
  89.5 0.0 copy-start.3
  89.5 3.4 %fusion.22 = bf16[2,768,192]{1,2,0:T(8,128)(2,1)} fusion(bf16[2,768,768]{2,1,0:T(8,128)(2,1)S(1)} %copy-done, f32[2,768,192]{1,2,0:T(8,128)} %get-tuple-element.7, f32[2,768,192]{1,2,0:T(8,128)S(1)} %get-tuple-element.6), kind=kOutput, calls=%fused_computation.19 | convolution fusion | flops 454164480 | bytes 5308416 | tf_op jit(solution)/shard_map/bij,bjk->bik/dot_general | solution.py:40
  92.9 0.0 copy-done.3
  92.9 0.0 all-gather.5.cloned.1.call-update
  92.9 48.9 %all-gather.5.cloned.1.call-done = bf16[2,768,768]{1,2,0:T(8,128)(2,1)} async-done(((bf16[2,768,192]{1,2,0:T(8,128)(2,1)}), bf16[2,768,768]{1,2,0:T(8,128)(2,1)}) %all-gather.5.cloned.1.call-update) | async-done | bytes 2359312 | tf_op jit(solution)/shard_map/all_gather | solution.py:46
  141.9 2.5 %convolution_convert_fusion = bf16[2,768,192]{1,2,0:T(8,128)(2,1)S(1)} fusion(bf16[2,768,768]{1,2,0:T(8,128)(2,1)} %all-gather.5.cloned.1.call-done, bf16[2,768,768]{2,1,0:T(8,128)(2,1)} %param.13, s32[]{:T(128)S(6)} %select_n.17), kind=kOutput, calls=%fused_computation.17 | convolution fusion | flops 453279744 | bytes 3538948 | tf_op jit(solution)/shard_map/bij,bkj->bik/dot_general | solution.py:44
  144.4 1.8 %copy.28 = bf16[2,768,192]{2,0,1:T(2,128)(2,1)} copy(bf16[2,768,192]{1,2,0:T(8,128)(2,1)S(1)} %convolution_convert_fusion) | data formatting | bytes 1179648 | tf_op jit(solution)/shard_map/convert_element_type | solution.py:50
  146.1 3.7 %all-to-all-start.1 = ((bf16[2,768,192]{2,0,1:T(2,128)(2,1)}), bf16[2,768,192]{2,0,1:T(2,128)(2,1)S(1)}, u32[]{:S(2)}, u32[]{:S(2)}) async-start(bf16[2,768,192]{2,0,1:T(2,128)(2,1)} %copy.28), calls=%async_computation.1 | async-start | bytes 1572864 | tf_op jit(solution)/shard_map/all_to_all | solution.py:51
  149.8 0.0 copy-start.1
  149.8 4.3 %fusion.13 = f32[2,768,192]{1,2,0:T(8,128)} fusion(bf16[2,768,192]{1,2,0:T(8,128)(2,1)} %all_to_all.29, bf16[2,768,768]{1,0,2:T(2,128)(2,1)} %all-gather.3.cloned.1.call-done, f32[2,768,192]{1,2,0:T(8,128)} %param.11, f32[]{:T(128)S(6)} %mul.74), kind=kOutput, calls=%fused_computation.14 | convolution fusion | flops 453869568 | bytes 5308420 | tf_op jit(solution)/shard_map/bji,bjk->bik/dot_general | solution.py:28
  154.1 0.0 copy-done.1
  154.1 0.0 copy-start.4
  154.1 1.3 constant_dynamic-slice_fusion
  155.4 0.0 copy-done.4
  155.4 1.7 fusion.16
  157.1 5.3 %all-to-all-done.1 = bf16[2,768,192]{2,0,1:T(2,128)(2,1)S(1)} async-done(((bf16[2,768,192]{2,0,1:T(2,128)(2,1)}), bf16[2,768,192]{2,0,1:T(2,128)(2,1)S(1)}, u32[]{:S(2)}, u32[]{:S(2)}) %all-to-all-start.1) | async-done | bytes 589856 | tf_op jit(solution)/shard_map/all_to_all | solution.py:51
  162.4 0.0 copy-start.2
  162.4 0.9 copy-done.2
  163.2 1.3 copy.29
  164.5 1.0 broadcast_in_dim.16
  165.5 2.7 %scatter_fusion = bf16[16,96,192]{2,1,0:T(8,128)(2,1)} fusion(bf16[16,96,192]{2,1,0:T(8,128)(2,1)} %broadcast_in_dim.16, s32[16]{0:T(128)S(1)} %compare_select_fusion, bf16[16,96,192]{2,1,0:T(8,128)(2,1)S(1)} %bitcast.21), kind=kCustom, calls=%fused_computation.1 | custom fusion | bytes 1769536 | tf_op jit(solution)/shard_map/scatter | solution.py:52
  (1 shorter events, 0.0 us)
Async XLA Ops:
  7.2 77.1 %copy-start = (bf16[2,768,768]{2,1,0:T(8,128)(2,1)S(1)}, bf16[2,768,768]{2,1,0:T(8,128)(2,1)}, u32[]{:S(2)}) copy-start(bf16[2,768,768]{2,1,0:T(8,128)(2,1)} %param.12) | copy-start | bytes 7077892
  7.2 77.1 %all-gather.3.cloned.1.call-start = ((), (), s32[]{:S(2)}) async-start(), calls=%async_computation.2 | async-start | bytes 2949120 | tf_op jit(solution)/shard_map/all_gather | solution.py:24
  33.8 108.1 %all-gather.5.cloned.1.call-start = ((), (), s32[]{:S(2)}) async-start(), calls=%async_computation.3 | async-start | bytes 2949120 | tf_op jit(solution)/shard_map/all_gather | solution.py:46
  89.5 3.4 %copy-start.3 = (f32[2,768,192]{1,2,0:T(8,128)}, f32[2,768,192]{1,2,0:T(8,128)S(1)}, u32[]{:S(2)}) copy-start(f32[2,768,192]{1,2,0:T(8,128)S(1)} %get-tuple-element.6) | copy-start | bytes 3538948
  146.1 16.2 %all-to-all-start.1 = ((bf16[2,768,192]{2,0,1:T(2,128)(2,1)}), bf16[2,768,192]{2,0,1:T(2,128)(2,1)S(1)}, u32[]{:S(2)}, u32[]{:S(2)}) async-start(bf16[2,768,192]{2,0,1:T(2,128)(2,1)} %copy.28), calls=%async_computation.1 | async-start | bytes 1572864 | tf_op jit(solution)/shard_map/all_to_all | solution.py:51
  149.8 4.3 %copy-start.1 = (bf16[2,768,768]{1,0,2:T(2,128)(2,1)S(1)}, bf16[2,768,768]{1,0,2:T(2,128)(2,1)}, u32[]{:S(2)}) copy-start(bf16[2,768,768]{1,0,2:T(2,128)(2,1)} %all-gather.3.cloned.1.call-done) | copy-start | bytes 7077892
  154.1 1.3 copy-start.4
  162.4 0.9 copy-start.2
Sparse Core Ops, SparseCore 0:
  33.9 50.3 all-gather.2
  93.0 48.7 all-gather.4
where the time goes:
time: 177 us; the launch traced here: 176 us
  blocking collectives  61 us (34%)
  waiting for transfers between devices  59.6 us (34%)
  matrix products  17 us (10%)
  local copies, waits for them, and re-layouts  16.2 us (9%)
  between operations  16 us (9%)
  starting transfers between devices  3.73 us (2%)
  other arithmetic  2.62 us (1%)
    all_gather x1, waiting for transfers between devices, body(): lax.all_gather(back, 'blk', axis=2, tiled=True)  48.9 us
    psum x1, blocking collectives, body(): total = lax.psum(partial_sum, ('fsdp', 'blk'))  43.4 us
    all_to_all x1, blocking collectives, body(): lax.all_to_all(arranged, 'fsdp', split_axis=0, concat_axis=1, tiled=True)  17.6 us
    all_to_all x3, local copies, waits for them, and re-layouts, body(): lax.all_to_all(arranged, 'fsdp', split_axis=0, concat_axis=1, tiled=True)  5.5 us
    all_gather x1, waiting for transfers between devices, body(): whole = lax.all_gather(owned, 'blk', axis=2, tiled=True)  5.34 us
    all_to_all x1, waiting for transfers between devices, body(): lax.all_to_all(stepped, 'fsdp', split_axis=1, concat_axis=0, tiled=True)  5.27 us
    dot_general x1, matrix products, body(): jnp.einsum('bji,bjk->bik', basis_left, turned, preferred_element_type=jnp...  5.16 us
    dot_general x1, matrix products, body(): jnp.einsum('bji,bjk->bik', whole, owned, preferred_element_type=jnp.float32)  4.26 us
  transfers between devices with their start and end apart: 3, of which 3 were waited for; matrix products, arithmetic and copies ran while one was open for 5% of the time, Pallas kernels for 0%

commit v1 on v0

--- a/solution.py
+++ b/solution.py
@@ -41,12 +41,38 @@
         "bij,bjk->bik", basis_left, scaled, preferred_element_type=jnp.float32
     ).astype(jnp.bfloat16)
     right_rows = lax.dynamic_slice_in_dim(basis_right, first_col, width, 1)
-    summed = jnp.einsum(
+    size, here, width_2 = (lax.axis_size("blk"), lax.axis_index("blk"), back.shape[2])
+    right = [(i, (i + 1) % size) for i in range(size)]
+    left = [(i, (i - 1) % size) for i in range(size)]
+    halfway = size // 2
+    from_left = from_right = back
+    total_2 = jnp.einsum(
         "bij,bkj->bik",
-        lax.all_gather(back, "blk", axis=2, tiled=True),
-        right_rows,
+        back,
+        lax.dynamic_slice_in_dim(right_rows, here * width_2, back.shape[2], axis=2),
         preferred_element_type=jnp.float32,
     )
+    for hop in range(1, halfway + 1):
+        from_left = lax.ppermute(from_left, "blk", right)
+        if hop < size - halfway:
+            from_right = lax.ppermute(from_right, "blk", left)
+            total_2 = total_2 + jnp.einsum(
+                "bij,bkj->bik",
+                from_right,
+                lax.dynamic_slice_in_dim(
+                    right_rows, (here + hop) % size * width_2, from_right.shape[2], axis=2
+                ),
+                preferred_element_type=jnp.float32,
+            )
+        total_2 = total_2 + jnp.einsum(
+            "bij,bkj->bik",
+            from_left,
+            lax.dynamic_slice_in_dim(
+                right_rows, (here - hop) % size * width_2, from_left.shape[2], axis=2
+            ),
+            preferred_element_type=jnp.float32,
+        )
+    summed = total_2
     stepped = summed.astype(jnp.bfloat16)
     returned = lax.all_to_all(stepped, "fsdp", split_axis=1, concat_axis=0, tiled=True)
     placed = jnp.zeros_like(returned).at[owner_slots].set(returned)

time: 177 us -> 169 us (0.955)
  waiting for transfers between devices: 59.6 us -> 46.8 us
  starting transfers between devices: 3.73 us -> 7.54 us
    all_gather x1 -> x0, waiting for transfers between devices: 48.9 us -> none  [body(): lax.all_gather(back, 'blk', axis=2, tiled=True)]
    ppermute x0 -> x3, waiting for transfers between devices: none -> 36.1 us  [the longest x2 26.6 us: body(): from_left = lax.ppermute(from_left, 'blk', right)]
    ppermute x0 -> x3, starting transfers between devices: none -> 3.83 us  [the longest x1 3.82 us: body(): from_right = lax.ppermute(from_right, 'blk', left)]
  transfers between devices with their start and end apart: 3 -> 5, of which waited for: 3 -> 5; matrix products, arithmetic and copies ran while one was open for 5% -> 6% of each run, Pallas kernels for 0% -> 0%
where the time goes in v1:
time: 169 us; the launch traced here: 168 us
  blocking collectives  61.1 us (36%)
  waiting for transfers between devices  46.8 us (28%)
  matrix products  18.3 us (11%)
  local copies, waits for them, and re-layouts  16.2 us (10%)
  between operations  16 us (9%)
  starting transfers between devices  7.54 us (4%)
  other arithmetic  2.62 us (2%)
    psum x1, blocking collectives, body(): total = lax.psum(partial_sum, ('fsdp', 'blk'))  43.5 us
    ppermute x2, waiting for transfers between devices, body(): from_left = lax.ppermute(from_left, 'blk', right)  26.6 us
    all_to_all x1, blocking collectives, body(): lax.all_to_all(arranged, 'fsdp', split_axis=0, concat_axis=1, tiled=True)  17.6 us
    ppermute x1, waiting for transfers between devices, body(): from_right = lax.ppermute(from_right, 'blk', left)  9.52 us
    all_to_all x3, local copies, waits for them, and re-layouts, body(): lax.all_to_all(arranged, 'fsdp', split_axis=0, concat_axis=1, tiled=True)  5.5 us
    dot_general x1, matrix products, body(): jnp.einsum('bji,bjk->bik', basis_left, turned, preferred_element_type=jnp...  5.5 us
    all_gather x1, waiting for transfers between devices, body(): whole = lax.all_gather(owned, 'blk', axis=2, tiled=True)  5.34 us
    all_to_all x1, waiting for transfers between devices, body(): lax.all_to_all(stepped, 'fsdp', split_axis=1, concat_axis=0, tiled=True)  5.27 us
  transfers between devices with their start and end apart: 5, of which 5 were waited for; matrix products, arithmetic and copies ran while one was open for 6% of the time, Pallas kernels for 0%

profile of v1, /device:TPU:0, one launch (start us, length us, event | category | flops | bytes accessed | tf_op | source)
XLA Modules:
  0.0 168.4 jit_solution(762076064847111056)
XLA Ops:
  7.2 0.0 copy-start
  7.2 0.0 all-gather.2.cloned.1.call-start
  7.2 0.8 compare_select_fusion
  8.0 0.7 compare_and_fusion
  8.7 1.7 %gather_fusion = bf16[16,96,192]{2,1,0:T(8,128)(2,1)S(1)} fusion(bf16[16,96,192]{2,1,0:T(8,128)(2,1)} %param.8, s32[1024]{0:T(1024)S(1)} %pad_clamp_fusion), kind=kCustom, calls=%fused_computation | custom fusion | bytes 1179712 | tf_op jit(solution)/shard_map/jit(_take)/gather | solution.py:15
  10.4 0.1 broadcast_select_fusion
  10.6 17.6 %all_to_all.36 = bf16[16,96,192]{2,1,0:T(8,128)(2,1)} all-to-all(bf16[16,96,192]{2,1,0:T(8,128)(2,1)S(1)} %broadcast_select_fusion), channel_id=1, replica_groups=mesh['fsdp'=8,'blk'=4] {'fsdp'}, dimensions={0} | all-to-all | bytes 1179648 | tf_op jit(solution)/shard_map/all_to_all | solution.py:16
  28.2 1.6 copy.24
  29.8 1.5 all_to_all.29
  31.2 2.5 %copy.25 = bf16[2,768,192]{1,0,2:T(2,128)(2,1)} copy(bf16[2,768,192]{1,2,0:T(8,128)(2,1)} %all_to_all.29) | data formatting | bytes 1179648 | tf_op jit(solution)/shard_map/all_to_all | solution.py:16
  33.7 0.0 all-gather.2.cloned.1.call-update
  33.8 1.0 multiply_reduce_fusion
  34.8 43.5 %psum.7 = f32[]{:T(128)} all-reduce(f32[]{:T(128)} %multiply_reduce_fusion), channel_id=1, replica_groups=mesh['fsdp'=8,'blk'=4] {'fsdp','blk'}, use_global_device_ids=true, to_apply=%region_1.2 | all-reduce | flops 1 | bytes 8 | tf_op jit(solution)/shard_map/psum | solution.py:21
  79.0 5.3 %all-gather.2.cloned.1.call-done = bf16[2,768,768]{1,0,2:T(2,128)(2,1)} async-done(((bf16[2,768,192]{1,0,2:T(2,128)(2,1)}), bf16[2,768,768]{1,0,2:T(2,128)(2,1)}) %all-gather.2.cloned.1.call-update) | async-done | bytes 2359312 | tf_op jit(solution)/shard_map/all_gather | solution.py:24
  84.3 0.0 copy-done
  84.3 5.5 %fusion.25 = (f32[2,768,192]{1,2,0:T(8,128)S(1)}, f32[2,768,192]{1,2,0:T(8,128)}) fusion(f32[2,768,192]{1,2,0:T(8,128)} %param.15, f32[2,768,192]{1,2,0:T(8,128)} %param.14, bf16[2,768,768]{2,1,0:T(8,128)(2,1)} %param.12, bf16[2,768,768]{1,0,2:T(2,128)(2,1)} %all-gather.2.cloned.1.call-done, bf16[2,768,768]{2,1,0:T(8,128)(2,1)S(1)} %copy-done, ...), kind=kOutput, calls=%fused_computation.22 | convolution fusion | flops 908623872 | bytes 10223624 | tf_op jit(solution)/shard_map/bji,bjk->bik/dot_general | solution.py:34
  89.8 0.0 copy-start.3
  89.8 4.2 %convolution_convert_fusion = bf16[2,192,768]{2,1,0:T(8,128)(2,1)} fusion(bf16[2,768,768]{2,1,0:T(8,128)(2,1)} %param.12, f32[2,768,192]{1,2,0:T(8,128)} %get-tuple-element.7, f32[2,768,192]{1,2,0:T(8,128)S(1)} %get-tuple-element.6), kind=kOutput, calls=%fused_computation.21 | convolution fusion | flops 454164480 | bytes 5308416 | tf_op jit(solution)/shard_map/bij,bjk->bik/dot_general | solution.py:40
  94.0 0.0 copy-done.3
  94.0 0.0 collective-permute-start.1
  94.0 3.8 %collective-permute-start = (bf16[2,768,192]{1,2,0:T(8,128)(2,1)}, bf16[2,768,192]{1,2,0:T(8,128)(2,1)S(1)}, u32[]{:S(2)}, u32[]{:S(2)}) collective-permute-start(bf16[2,768,192]{1,2,0:T(8,128)(2,1)} %bitcast.3), channel_id=1, source_target_pairs={{0,3},{1,0},{2,1},{3,2},{4,7},{5,4},{6,5},{7,6},{8,11},{9,8},{10,9... | collective-permute-start | bytes 1769480 | tf_op jit(solution)/shard_map/ppermute | solution.py:58
  97.8 1.5 fusion.33
  99.3 12.9 %collective-permute-done.1 = bf16[2,768,192]{1,2,0:T(8,128)(2,1)S(1)} collective-permute-done((bf16[2,768,192]{1,2,0:T(8,128)(2,1)}, bf16[2,768,192]{1,2,0:T(8,128)(2,1)S(1)}, u32[]{:S(2)}, u32[]{:S(2)}) %collective-permute-start.1) | collective-permute-done | bytes 589856 | tf_op jit(solution)/shard_map/ppermute | solution.py:56
  112.2 0.0 collective-permute-start.2
  112.2 9.5 %collective-permute-done = bf16[2,768,192]{1,2,0:T(8,128)(2,1)S(1)} collective-permute-done((bf16[2,768,192]{1,2,0:T(8,128)(2,1)}, bf16[2,768,192]{1,2,0:T(8,128)(2,1)S(1)}, u32[]{:S(2)}, u32[]{:S(2)}) %collective-permute-start) | collective-permute-done | bytes 589856 | tf_op jit(solution)/shard_map/ppermute | solution.py:58
  121.7 0.4 convolution_add_fusion.2
  122.1 0.4 convolution_add_fusion.1
  122.5 13.7 %collective-permute-done.2 = bf16[2,768,192]{1,2,0:T(8,128)(2,1)S(1)} collective-permute-done((bf16[2,768,192]{1,2,0:T(8,128)(2,1)S(1)}, bf16[2,768,192]{1,2,0:T(8,128)(2,1)S(1)}, u32[]{:S(2)}, u32[]{:S(2)}) %collective-permute-start.2) | collective-permute-done | bytes 589856 | tf_op jit(solution)/shard_map/ppermute | solution.py:56
  136.2 0.4 fusion.19
  136.6 1.8 %copy.28 = bf16[2,768,192]{2,0,1:T(2,128)(2,1)} copy(bf16[2,768,192]{1,2,0:T(8,128)(2,1)S(1)} %fusion.19) | data formatting | bytes 1179648 | tf_op jit(solution)/shard_map/convert_element_type | solution.py:76
  138.4 3.7 %all-to-all-start.1 = ((bf16[2,768,192]{2,0,1:T(2,128)(2,1)}), bf16[2,768,192]{2,0,1:T(2,128)(2,1)S(1)}, u32[]{:S(2)}, u32[]{:S(2)}) async-start(bf16[2,768,192]{2,0,1:T(2,128)(2,1)} %copy.28), calls=%async_computation.1 | async-start | bytes 1572864 | tf_op jit(solution)/shard_map/all_to_all | solution.py:77
  142.1 0.0 copy-start.1
  142.1 4.3 %fusion.13 = f32[2,768,192]{1,2,0:T(8,128)} fusion(bf16[2,768,192]{1,2,0:T(8,128)(2,1)} %all_to_all.29, bf16[2,768,768]{1,0,2:T(2,128)(2,1)} %all-gather.2.cloned.1.call-done, f32[2,768,192]{1,2,0:T(8,128)} %param.11, f32[]{:T(128)S(6)} %mul.87), kind=kOutput, calls=%fused_computation.17 | convolution fusion | flops 453869568 | bytes 5308420 | tf_op jit(solution)/shard_map/bji,bjk->bik/dot_general | solution.py:28
  146.3 0.0 copy-done.1
  146.3 0.0 copy-start.4
  146.3 1.3 constant_dynamic-slice_fusion
  147.6 0.0 copy-done.4
  147.7 1.7 %fusion.16 = f32[2,768,192]{1,2,0:T(8,128)} fusion(bf16[2,768,768]{1,0,2:T(2,128)(2,1)S(1)} %copy-done.1, f32[2,768,192]{1,2,0:T(8,128)S(1)} %copy-done.4, bf16[2,192,768]{1,0,2:T(2,128)(2,1)S(1)} %constant_dynamic-slice_fusion, f32[]{:T(128)S(6)} %mul.87), kind=kOutput, calls=%fused_computation.18 | convolution fusion | flops 453869568 | bytes 5308420 | tf_op jit(solution)/shard_map/bij,bkj->bik/dot_general | solution.py:27
  149.4 5.3 %all-to-all-done.1 = bf16[2,768,192]{2,0,1:T(2,128)(2,1)S(1)} async-done(((bf16[2,768,192]{2,0,1:T(2,128)(2,1)}), bf16[2,768,192]{2,0,1:T(2,128)(2,1)S(1)}, u32[]{:S(2)}, u32[]{:S(2)}) %all-to-all-start.1) | async-done | bytes 589856 | tf_op jit(solution)/shard_map/all_to_all | solution.py:77
  154.6 0.0 copy-start.2
  154.6 0.9 copy-done.2
  155.5 1.3 copy.29
  156.8 1.0 broadcast_in_dim.16
  157.7 2.7 %scatter_fusion = bf16[16,96,192]{2,1,0:T(8,128)(2,1)} fusion(bf16[16,96,192]{2,1,0:T(8,128)(2,1)} %broadcast_in_dim.16, s32[16]{0:T(128)S(1)} %compare_select_fusion, bf16[16,96,192]{2,1,0:T(8,128)(2,1)S(1)} %bitcast.22), kind=kCustom, calls=%fused_computation.1 | custom fusion | bytes 1769536 | tf_op jit(solution)/shard_map/scatter | solution.py:78
  (1 shorter events, 0.0 us)
Async XLA Ops:
  7.2 77.1 %copy-start = (bf16[2,768,768]{2,1,0:T(8,128)(2,1)S(1)}, bf16[2,768,768]{2,1,0:T(8,128)(2,1)}, u32[]{:S(2)}) copy-start(bf16[2,768,768]{2,1,0:T(8,128)(2,1)} %param.13) | copy-start | bytes 7077892
  7.2 77.1 %all-gather.2.cloned.1.call-start = ((), (), s32[]{:S(2)}) async-start(), calls=%async_computation.2 | async-start | bytes 2949120 | tf_op jit(solution)/shard_map/all_gather | solution.py:24
  89.8 4.2 %copy-start.3 = (f32[2,768,192]{1,2,0:T(8,128)}, f32[2,768,192]{1,2,0:T(8,128)S(1)}, u32[]{:S(2)}) copy-start(f32[2,768,192]{1,2,0:T(8,128)S(1)} %get-tuple-element.6) | copy-start | bytes 3538948
  94.0 18.2 %collective-permute-start.1 = (bf16[2,768,192]{1,2,0:T(8,128)(2,1)}, bf16[2,768,192]{1,2,0:T(8,128)(2,1)S(1)}, u32[]{:S(2)}, u32[]{:S(2)}) collective-permute-start(bf16[2,768,192]{1,2,0:T(8,128)(2,1)} %bitcast.3), channel_id=1, source_target_pairs={{0,1},{1,2},{2,3},{3,0},{4,5},{5,6},{6,7},{7,4},{8,9},{9,10},{10,1... | collective-permute-start | bytes 1769480 | tf_op jit(solution)/shard_map/ppermute | solution.py:56
  94.0 27.7 %collective-permute-start = (bf16[2,768,192]{1,2,0:T(8,128)(2,1)}, bf16[2,768,192]{1,2,0:T(8,128)(2,1)S(1)}, u32[]{:S(2)}, u32[]{:S(2)}) collective-permute-start(bf16[2,768,192]{1,2,0:T(8,128)(2,1)} %bitcast.3), channel_id=1, source_target_pairs={{0,3},{1,0},{2,1},{3,2},{4,7},{5,4},{6,5},{7,6},{8,11},{9,8},{10,9... | collective-permute-start | bytes 1769480 | tf_op jit(solution)/shard_map/ppermute | solution.py:58
  112.2 24.0 %collective-permute-start.2 = (bf16[2,768,192]{1,2,0:T(8,128)(2,1)S(1)}, bf16[2,768,192]{1,2,0:T(8,128)(2,1)S(1)}, u32[]{:S(2)}, u32[]{:S(2)}) collective-permute-start(bf16[2,768,192]{1,2,0:T(8,128)(2,1)S(1)} %collective-permute-done.1), channel_id=1, source_target_pairs={{0,1},{1,2},{2,3},{3,0},{4,5},{5,6},{6,7},{7,4},{8,9},{9,10},{10,1... | collective-permute-start | bytes 1769480 | tf_op jit(solution)/shard_map/ppermute | solution.py:56
  138.4 16.2 %all-to-all-start.1 = ((bf16[2,768,192]{2,0,1:T(2,128)(2,1)}), bf16[2,768,192]{2,0,1:T(2,128)(2,1)S(1)}, u32[]{:S(2)}, u32[]{:S(2)}) async-start(bf16[2,768,192]{2,0,1:T(2,128)(2,1)} %copy.28), calls=%async_computation.1 | async-start | bytes 1572864 | tf_op jit(solution)/shard_map/all_to_all | solution.py:77
  142.1 4.3 %copy-start.1 = (bf16[2,768,768]{1,0,2:T(2,128)(2,1)S(1)}, bf16[2,768,768]{1,0,2:T(2,128)(2,1)}, u32[]{:S(2)}) copy-start(bf16[2,768,768]{1,0,2:T(2,128)(2,1)} %all-gather.2.cloned.1.call-done) | copy-start | bytes 7077892
  146.3 1.3 copy-start.4
  154.6 0.9 copy-start.2
Sparse Core Ops, SparseCore 0:
  33.9 50.3 all-gather.1
